TPU v7x, 128 devices: a whole 4x4x4 slice. The times are simulated.
128 devices in a mesh: req: 4 (over x), tp: 32 (over z, y, core).
Axes of the slice: x: 4, y: 4, z: 4, core: 2. Of those that a mesh axis runs over, the one named last changes fastest.
Arguments:
- step_inputs: bfloat16 [4, 256, 1536], P(None, ('req', 'tp')), may hold values from -6 to 6
- qkv_weight: bfloat16 [1536, 2048], replicated, may hold values from -0.15625 to 0.15625
- qkv_bias: float32 [2048], replicated, may hold values from -8 to 8
- out_weight: bfloat16 [1536, 1536], P('tp'), may hold values from -0.15625 to 0.15625
- gate_weight: bfloat16 [1536, 8960], P(None, 'tp'), may hold values from -0.15625 to 0.15625
- up_weight: bfloat16 [1536, 8960], P(None, 'tp'), may hold values from -0.15625 to 0.15625
- down_weight: bfloat16 [8960, 1536], P('tp'), may hold values from -0.0625 to 0.0625
- cache_keys: bfloat16 [256, 4096, 256], P(('req', 'tp')), may hold values from -60 to 60
- cache_values: bfloat16 [256, 4096, 256], P(('req', 'tp')), may hold values from -24 to 24
- lengths: int32 [32, 8], replicated, may hold values from 1 to 4096, as said below
- parents: int32 [4, 32, 8], replicated, may hold values from 0 to 7
- slot_request: int32 [32], replicated, may hold values from 0 to 31, each once
Outputs:
- outputs: bfloat16 [4, 256, 1536], P(None, ('req', 'tp'))
Inputs may be any that keep to these rules, and one draw needn't show every extreme that they name: lengths[r, c] is the number of cached positions of beam c of request r; some beam has exactly 4096. parents[t, r, b] names a beam of the same request r. `slot_request`: a permutation of the requests; slots 8 * i to 8 * i + 7 are rows of index i of req.
All inputs are finite; a program needn't handle non-finite values.
Results may differ from a plain program's by a relative error of at most 0.022.
The roundings to bfloat16 on the way count: a program that leaves them out, or rounds other values in their place, can miss the bound.
Values may be sent and summed in bfloat16 or wider, within the bound.
No kernel may reach another device: no remote copies, remote signals or barrier semaphores. Data moves between devices by JAX's collectives and lax.ppermute only.
A program may use at most 128 MiB of HBM per device.

v0:
```python
import jax
import jax.numpy as jnp
from jax import lax
from jax.sharding import PartitionSpec as P

Q_HEADS = 12
KV_HEADS = 2
theta_base = 1000000.0
norm_eps = 1e-06
masked_score = -1e30


def rms_normed(values):
    values = values.astype(jnp.float32)
    factor = lax.rsqrt(jnp.mean(values * values, axis=-1, keepdims=True) + norm_eps)
    return (values * factor).astype(jnp.bfloat16)


def rotate(vectors, positions):
    half = vectors.shape[-1] // 2
    freqs = theta_base ** (-jnp.arange(half, dtype=jnp.float32) * 2.0 / vectors.shape[-1])
    angles = positions.astype(jnp.float32)[:, None] * freqs[None, :]
    cosine = jnp.cos(angles)[:, None, :]
    sine = jnp.sin(angles)[:, None, :]
    values = vectors.astype(jnp.float32)
    first = values[..., :half]
    second = values[..., half:]
    return jnp.concatenate(
        [first * cosine - second * sine, second * cosine + first * sine], axis=-1
    ).astype(jnp.bfloat16)


def owner_rows(flat, owned_count, beams, inverse):
    owned_global = flat * owned_count + jnp.arange(owned_count, dtype=jnp.int32)
    owned_request = owned_global // beams
    owned_beam = owned_global % beams
    beam_range = jnp.arange(beams, dtype=jnp.int32)
    query_rows = (inverse[owned_request][:, None] * beams + beam_range[None, :]).reshape(-1)
    return (owned_request, owned_beam, query_rows)


def owned_attention(
    every_query, keys, values, owned_request, owned_beam, query_rows, root_all, lengths
):
    owned_rows, context, kv_width = keys.shape
    beams = root_all.shape[1]
    head_dim = kv_width // KV_HEADS
    group = Q_HEADS // KV_HEADS
    grouped = jnp.take(every_query, query_rows, axis=0).reshape(
        owned_rows, beams, KV_HEADS, group, head_dim
    )
    keys = keys.reshape(owned_rows, context, KV_HEADS, head_dim)
    values = values.reshape(owned_rows, context, KV_HEADS, head_dim)
    scores = jnp.einsum(
        "jbkgd,jpkd->jbkgp", grouped, keys, preferred_element_type=jnp.float32
    ) * head_dim ** (-0.5)
    limits = lengths[owned_request, owned_beam]
    live = (jnp.arange(context, dtype=jnp.int32)[None, :] < limits[:, None])[:, None, None, None, :]
    scores = jnp.where(live, scores, masked_score)
    peak = jnp.max(scores, axis=-1)
    weights = jnp.where(live, jnp.exp(scores - peak[..., None]), 0.0)
    total = jnp.sum(weights, axis=-1)
    output = jnp.einsum(
        "jbkgp,jpkd->jbkgd",
        weights.astype(jnp.bfloat16),
        values,
        preferred_element_type=jnp.float32,
    )
    chosen = (root_all[owned_request] == owned_beam[:, None])[:, :, None, None]
    peak = jnp.where(chosen, peak, 0.0).reshape(owned_rows * beams, KV_HEADS, group)
    total = jnp.where(chosen, total, 0.0).reshape(owned_rows * beams, KV_HEADS, group)
    output = jnp.where(chosen[..., None], output, 0.0).reshape(
        owned_rows * beams, KV_HEADS, group, head_dim
    )
    return (peak, total, output)


def spread_rows(pieces, target_rows, row_count):
    return tuple(
        (
            jnp.zeros((row_count,) + piece.shape[1:], jnp.float32).at[target_rows].add(piece)
            for piece in pieces
        )
    )


def per_device(
    step_inputs,
    qkv_weight,
    qkv_bias,
    out_weight,
    gate_weight,
    up_weight,
    down_weight,
    cache_keys,
    cache_values,
    lengths,
    parents,
    slot_request,
):
    steps_count, rows_dev, width = step_inputs.shape
    beams = parents.shape[2]
    requests = slot_request.shape[0]
    req_count = lax.axis_size("req")
    tp_count = lax.axis_size("tp")
    group_requests = requests // req_count
    group_rows = group_requests * beams
    total_rows = requests * beams
    owned_count = cache_keys.shape[0]
    kv_width = cache_keys.shape[2]
    head_dim = kv_width // KV_HEADS
    group = Q_HEADS // KV_HEADS
    attn_width = Q_HEADS * head_dim
    req_index = lax.axis_index("req")
    tp_index = lax.axis_index("tp")
    flat_index = req_index * tp_count + tp_index
    my_requests = lax.dynamic_slice_in_dim(slot_request, req_index * group_requests, group_requests)
    inverse = (
        jnp.zeros((requests,), jnp.int32)
        .at[slot_request]
        .set(jnp.arange(requests, dtype=jnp.int32))
    )
    owned_request, owned_beam, query_rows = owner_rows(flat_index, owned_count, beams, inverse)
    beam_range = jnp.arange(beams, dtype=jnp.int32)
    root_all = jnp.broadcast_to(beam_range[None, :], (requests, beams))
    gen_keys = jnp.zeros((steps_count, group_rows, kv_width), jnp.bfloat16)
    gen_values = jnp.zeros((steps_count, group_rows, kv_width), jnp.bfloat16)
    base_rows = (jnp.arange(group_requests, dtype=jnp.int32) * beams)[:, None]
    column_width = out_weight.shape[0]
    results = []
    for step in range(steps_count):
        root_all = jnp.take_along_axis(root_all, parents[step], axis=1)
        reorder = (base_rows + parents[step][my_requests]).reshape(-1)
        gen_keys = jnp.take(gen_keys, reorder, axis=1)
        gen_values = jnp.take(gen_values, reorder, axis=1)
        inputs = step_inputs[step]
        normed = rms_normed(inputs)
        qkv = (
            jnp.dot(
                lax.all_gather(normed, "tp", axis=0, tiled=True),
                qkv_weight,
                preferred_element_type=jnp.float32,
            )
            + qkv_bias
        ).astype(jnp.bfloat16)
        my_roots = root_all[my_requests]
        positions = (jnp.take_along_axis(lengths[my_requests], my_roots, axis=1) + step).reshape(-1)
        queries = rotate(qkv[:, :attn_width].reshape(group_rows, Q_HEADS, head_dim), positions)
        new_keys = rotate(
            qkv[:, attn_width : attn_width + kv_width].reshape(group_rows, KV_HEADS, head_dim),
            positions,
        )
        gen_keys = gen_keys.at[step].set(new_keys.reshape(group_rows, kv_width))
        gen_values = gen_values.at[step].set(qkv[:, attn_width + kv_width :])
        every_query = lax.all_gather(
            queries.reshape(group_rows, attn_width), "req", axis=0, tiled=True
        )
        part_peak, part_total, part_output = owned_attention(
            every_query,
            cache_keys,
            cache_values,
            owned_request,
            owned_beam,
            query_rows,
            root_all,
            lengths,
        )
        all_peak, all_total, all_output = spread_rows(
            (part_peak, part_total, part_output), query_rows, total_rows
        )
        sum_peak, sum_total, sum_output = lax.psum((all_peak, all_total, all_output), ("req", "tp"))
        peak = lax.dynamic_slice_in_dim(sum_peak, req_index * group_rows, group_rows, 0)
        total = lax.dynamic_slice_in_dim(sum_total, req_index * group_rows, group_rows, 0)
        output = lax.dynamic_slice_in_dim(sum_output, req_index * group_rows, group_rows, 0)
        grouped = queries.reshape(group_rows, KV_HEADS, group, head_dim)
        past_keys = gen_keys[: step + 1].reshape(step + 1, group_rows, KV_HEADS, head_dim)
        past_values = gen_values[: step + 1].reshape(step + 1, group_rows, KV_HEADS, head_dim)
        recent_scores = jnp.einsum(
            "bkgd,sbkd->bkgs", grouped, past_keys, preferred_element_type=jnp.float32
        ) * head_dim ** (-0.5)
        top = jnp.maximum(peak, jnp.max(recent_scores, axis=-1))
        factor = jnp.exp(peak - top)
        recent_weights = jnp.exp(recent_scores - top[..., None])
        denominator = total * factor + jnp.sum(recent_weights, axis=-1)
        numerator = output * factor[..., None] + jnp.einsum(
            "bkgs,sbkd->bkgd",
            recent_weights.astype(jnp.bfloat16),
            past_values,
            preferred_element_type=jnp.float32,
        )
        attention = (
            (numerator / denominator[..., None])
            .reshape(group_rows, attn_width)
            .astype(jnp.bfloat16)
        )
        columns = lax.dynamic_slice_in_dim(attention, tp_index * column_width, column_width, 1)
        attended = lax.psum_scatter(
            jnp.dot(columns, out_weight, preferred_element_type=jnp.float32).astype(jnp.bfloat16),
            "tp",
            scatter_dimension=0,
            tiled=True,
        ).astype(jnp.float32)
        middle = inputs.astype(jnp.float32) + attended
        mixed_in = rms_normed(middle)
        piece = lax.all_gather(mixed_in, "tp", axis=0, tiled=True)
        gate = jnp.dot(piece, gate_weight, preferred_element_type=jnp.float32)
        upward = jnp.dot(piece, up_weight, preferred_element_type=jnp.float32)
        hidden = (jax.nn.silu(gate) * upward).astype(jnp.bfloat16)
        lowered = lax.psum_scatter(
            jnp.dot(hidden, down_weight, preferred_element_type=jnp.float32).astype(jnp.bfloat16),
            "tp",
            scatter_dimension=0,
            tiled=True,
        ).astype(jnp.float32)
        results.append((middle + lowered).astype(jnp.bfloat16))
    return jnp.stack(results)


def solution(mesh):
    in_specs = (
        P(None, ("req", "tp"), None),
        P(),
        P(),
        P("tp", None),
        P(None, "tp"),
        P(None, "tp"),
        P("tp", None),
        P(("req", "tp"), None, None),
        P(("req", "tp"), None, None),
        P(),
        P(),
        P(),
    )
    out_specs = P(None, ("req", "tp"), None)
    return jax.shard_map(
        per_device, mesh=mesh, in_specs=in_specs, out_specs=out_specs, check_vma=False
    )
```

profile of v0, /device:TPU:1, one launch (start us, length us, event | category | flops | bytes accessed | tf_op | source)
XLA Modules:
  0.0 1172.3 jit_solution(9988134711650191990)
XLA Ops:
  9.8 1.9 gather_fusion.15
  12.0 1.9 gather_fusion.18
  15.5 1.9 gather_fusion.24
  18.3 1.9 gather_fusion.29
  28.1 27.6 %all-gather = bf16[32,2,1536]{2,1,0:T(2,128)(2,1)S(1)} all-gather(bf16[1,2,1536]{2,1,0:T(2,128)(2,1)S(1)} %fusion.170), channel_id=1, replica_groups=mesh['req'=4,'tp'=32] {'tp'}, dimensions={0}, use_global_device_ids=true | all-gather | bytes 202752 | tf_op jit(solution)/shard_map/all_gather | solution.py:140
  55.8 4.0 fusion.28
  61.5 12.0 %all_gather.37 = bf16[256,1536]{1,0:T(8,128)(2,1)S(1)} all-gather(bf16[64,1536]{1,0:T(8,128)(2,1)S(1)} %bitcast.314), channel_id=1, replica_groups=mesh['req'=4,'tp'=32] {'req'}, dimensions={0}, use_global_device_ids=true | all-gather | bytes 983040 | tf_op jit(solution)/shard_map/all_gather | solution.py:155
  74.2 7.0 reshape.1079
  81.2 6.9 reshape.1080
  88.8 4.0 fusion.204
  98.9 2.6 fusion.20
  108.8 67.0 %all-reduce.9 = (f32[256,2,6]{0,1,2:T(2,128)S(1)}, f32[256,2,6]{0,1,2:T(2,128)S(1)}) all-reduce(f32[256,2,6]{0,1,2:T(2,128)S(1)} %copy.328, f32[256,2,6]{0,1,2:T(2,128)S(1)} %copy.335), channel_id=1, replica_groups=mesh['req'=4,'tp'=32] {'req','tp'}, use_global_device_ids=true, to_apply=%region_6.10 | all-reduce | flops 6144 | bytes 49152 | tf_op jit(solution)/shard_map/psum | solution.py:171
  185.9 63.2 %all-reduce.20.cloned.1.call-done = f32[256,2,6,128]{3,1,2,0:T(2,128)} async-done(((f32[256,2,6,128]{3,1,2,0:T(2,128)}), f32[256,2,6,128]{3,1,2,0:T(2,128)}) %all-reduce.20.cloned.1.call-update) | async-done | bytes 1572880 | tf_op jit(solution)/shard_map/psum | solution.py:171
  249.1 2.9 fusion.98
  253.4 98.8 %all-reduce.22.cloned.1.call-done = bf16[64,1536]{1,0:T(8,128)(2,1)} async-done(((bf16[64,1536]{1,0:T(8,128)(2,1)}), bf16[64,1536]{1,0:T(8,128)(2,1)}) %all-reduce.22.cloned.1.call-update) | async-done | bytes 196624
  354.6 24.5 %all-gather.4 = bf16[32,2,1536]{2,1,0:T(2,128)(2,1)S(1)} all-gather(bf16[1,2,1536]{2,1,0:T(2,128)(2,1)S(1)} %get-tuple-element.172), channel_id=1, replica_groups=mesh['req'=4,'tp'=32] {'tp'}, dimensions={0}, use_global_device_ids=true | all-gather | bytes 202752 | tf_op jit(solution)/shard_map/all_gather | solution.py:140
  379.1 4.0 fusion.30
  383.8 23.3 %all-gather.2 = bf16[32,2,1536]{2,1,0:T(2,128)(2,1)S(1)} all-gather(bf16[1,2,1536]{2,1,0:T(2,128)(2,1)S(1)} %get-tuple-element.171), channel_id=1, replica_groups=mesh['req'=4,'tp'=32] {'tp'}, dimensions={0}, use_global_device_ids=true | all-gather | bytes 202752 | tf_op jit(solution)/shard_map/all_gather | solution.py:140
  407.2 4.0 fusion.29
  414.6 23.7 %all-gather.6 = bf16[32,2,1536]{2,1,0:T(2,128)(2,1)S(1)} all-gather(bf16[1,2,1536]{2,1,0:T(2,128)(2,1)S(1)} %get-tuple-element.173), channel_id=1, replica_groups=mesh['req'=4,'tp'=32] {'tp'}, dimensions={0}, use_global_device_ids=true | all-gather | bytes 202752 | tf_op jit(solution)/shard_map/all_gather | solution.py:140
  438.5 4.0 fusion.31
  443.4 11.9 %all_gather.46 = bf16[256,1536]{1,0:T(8,128)(2,1)S(1)} all-gather(bf16[64,1536]{1,0:T(8,128)(2,1)S(1)} %bitcast.315), channel_id=1, replica_groups=mesh['req'=4,'tp'=32] {'req'}, dimensions={0}, use_global_device_ids=true | all-gather | bytes 983040 | tf_op jit(solution)/shard_map/all_gather | solution.py:155
  458.1 10.9 all_gather.40
  470.6 11.8 %all_gather.43 = bf16[256,1536]{1,0:T(8,128)(2,1)S(1)} all-gather(bf16[64,1536]{1,0:T(8,128)(2,1)S(1)} %bitcast.317), channel_id=1, replica_groups=mesh['req'=4,'tp'=32] {'req'}, dimensions={0}, use_global_device_ids=true | all-gather | bytes 983040 | tf_op jit(solution)/shard_map/all_gather | solution.py:155
  484.1 4.0 fusion.206
  488.1 1.6 fusion.207
  492.0 1.7 fusion.83
  493.7 1.7 fusion.93
  495.4 2.1 fusion.22
  497.6 1.7 fusion.73
  520.4 1.6 copy.365
  527.6 1.6 copy.343
  539.2 1.8 copy.348
  549.3 1.9 select_bitcast_fusion
  551.3 30.5 %all-gather.1 = bf16[32,2,1536]{2,1,0:T(2,128)(2,1)S(1)} all-gather(bf16[1,2,1536]{2,1,0:T(2,128)(2,1)S(1)} %copy-done.66), channel_id=1, replica_groups=mesh['req'=4,'tp'=32] {'tp'}, dimensions={0}, use_global_device_ids=true | all-gather | bytes 202752 | tf_op jit(solution)/shard_map/all_gather | solution.py:205
  581.9 2.2 scatter.55
  588.9 119.1 %all-reduce.24.cloned.1.call-done = (f32[256,2,6]{2,1,0:T(2,128)}, f32[256,2,6]{2,1,0:T(2,128)}, f32[256,2,6]{2,1,0:T(2,128)}, f32[256,2,6]{2,1,0:T(2,128)}, f32[256,2,6]{2,1,0:T(2,128)}, /*index=5*/f32[256,2,6]{2,1,0:T(2,128)}) async-done(((f32[256,2,6]{2,1,0:T(2,128)}, f32[256,2,6]{2,1,0:T(2,128)}, f32[256,2,6]{2,1,0:T(2,128)}, f32[256,2,6]{2,1,0:T(2,128)}, f32[256,2,6]{2,1,0:T(2,128)}, ...) | async-done | bytes 73744 | tf_op jit(solution)/shard_map/psum | solution.py:171
  715.0 154.8 %all-reduce.26.cloned.1.call-done = (f32[256,2,6,128]{3,2,1,0:T(8,128)}, f32[256,2,6,128]{3,2,1,0:T(8,128)}, f32[256,2,6,128]{3,2,1,0:T(8,128)}) async-done(((f32[256,2,6,128]{3,2,1,0:T(8,128)}, f32[256,2,6,128]{3,2,1,0:T(8,128)}, f32[256,2,6,128]{3,2,1,0:T(8,128)}), (f32[256,2,6,128]{3,2,1,0:T(8,128)}, f32[256,2,6,128]{3,2,1,0:T(8,128)}, f32[256,2,6,128]{3,2,1,0:T(8,128)})) %all-reduce.26.cloned.1.call-update) | async-done | bytes 4718608 | tf_op jit(solution)/shard_map/psum | solution.py:171
  875.4 1.7 fusion.53
  878.8 1.6 convolution_convert_fusion.6
  880.4 100.5 %all-reduce.30.cloned.1.call-done = (bf16[64,1536]{1,0:T(8,128)(2,1)}, bf16[64,1536]{1,0:T(8,128)(2,1)}, bf16[64,1536]{1,0:T(8,128)(2,1)}) async-done(((bf16[64,1536]{1,0:T(8,128)(2,1)}, bf16[64,1536]{1,0:T(8,128)(2,1)}, bf16[64,1536]{1,0:T(8,128)(2,1)}), (bf16[64,1536]{1,0:T(8,128)(2,1)}, bf16[64,1536]{1,0:T(8,128)(2,1)}, bf16[64,1536]{1,0:T(8,128)(2,1)})) %all-reduce.30.cloned.1.call-update) | async-done | bytes 589840
  982.8 24.9 %all-gather.3 = bf16[32,2,1536]{2,1,0:T(2,128)(2,1)S(1)} all-gather(bf16[1,2,1536]{2,1,0:T(2,128)(2,1)S(1)} %get-tuple-element.174), channel_id=1, replica_groups=mesh['req'=4,'tp'=32] {'tp'}, dimensions={0}, use_global_device_ids=true | all-gather | bytes 202752 | tf_op jit(solution)/shard_map/all_gather | solution.py:205
  1008.2 1.6 convolution_convert_fusion.4
  1009.9 22.5 %all-gather.5 = bf16[32,2,1536]{2,1,0:T(2,128)(2,1)S(1)} all-gather(bf16[1,2,1536]{2,1,0:T(2,128)(2,1)S(1)} %get-tuple-element.176), channel_id=1, replica_groups=mesh['req'=4,'tp'=32] {'tp'}, dimensions={0}, use_global_device_ids=true | all-gather | bytes 202752 | tf_op jit(solution)/shard_map/all_gather | solution.py:205
  1032.9 1.6 convolution_convert_fusion.2
  1034.5 24.1 %all-gather.7 = bf16[32,2,1536]{2,1,0:T(2,128)(2,1)S(1)} all-gather(bf16[1,2,1536]{2,1,0:T(2,128)(2,1)S(1)} %get-tuple-element.175), channel_id=1, replica_groups=mesh['req'=4,'tp'=32] {'tp'}, dimensions={0}, use_global_device_ids=true | all-gather | bytes 202752 | tf_op jit(solution)/shard_map/all_gather | solution.py:205
  1059.1 1.7 convolution_convert_fusion
  1060.8 102.6 %all-reduce.28.cloned.1.call-done = (bf16[64,1536]{1,0:T(8,128)(2,1)}, bf16[64,1536]{1,0:T(8,128)(2,1)}, bf16[64,1536]{1,0:T(8,128)(2,1)}, bf16[64,1536]{1,0:T(8,128)(2,1)}) async-done(((bf16[64,1536]{1,0:T(8,128)(2,1)}, bf16[64,1536]{1,0:T(8,128)(2,1)}, bf16[64,1536]{1,0:T(8,128)(2,1)}, bf16[64,1536]{1,0:T(8,128)(2,1)}), (bf16[64,1536]{1,0:T(8,128)(2,1)}, bf16[64,1536]{1,0:T(8,128)(2,1)}, ...) | async-done | bytes 786448
  (478 shorter events, 124.4 us)
Async XLA Ops:
  6.5 872.2 %copy-start = (bf16[280,1536]{1,0:T(8,128)(2,1)S(1)}, bf16[280,1536]{1,0:T(8,128)(2,1)}, u32[]{:S(2)}) copy-start(bf16[280,1536]{1,0:T(8,128)(2,1)} %param.42) | copy-start | bytes 2580484
  6.5 242.6 %all-reduce.20.cloned.1.call-start = ((), (), s32[]{:S(2)}) async-start(), calls=%async_computation | async-start | bytes 3145728 | tf_op jit(solution)/shard_map/psum | solution.py:171
  8.8 79.9 %copy-start.68 = (pred[16]{0:T(512)(128)(4,1)}, pred[16]{0:T(512)(128)(4,1)S(1)}, u32[]{:S(2)}) copy-start(pred[16]{0:T(512)(128)(4,1)S(1)} %compare_and_fusion.4) | copy-start | bytes 52
  26.7 29.1 %copy-start.53 = (f32[2048]{0:T(1024)S(1)}, f32[2048]{0:T(1024)}, u32[]{:S(2)}) copy-start(f32[2048]{0:T(1024)} %param.38) | copy-start | bytes 24580
  61.0 20.2 %copy-start.42 = (f32[64,64]{1,0:T(8,128)}, f32[64,64]{1,0:T(8,128)S(1)}, u32[]{:S(2)}) copy-start(f32[64,64]{1,0:T(8,128)S(1)} %get-tuple-element.217) | copy-start | bytes 49156
  61.0 20.2 %copy-start.44 = (f32[64,64]{1,0:T(8,128)}, f32[64,64]{1,0:T(8,128)S(1)}, u32[]{:S(2)}) copy-start(f32[64,64]{1,0:T(8,128)S(1)} %get-tuple-element.218) | copy-start | bytes 49156
  73.5 14.6 %copy-start.67 = (s32[1024]{0:T(1024)}, s32[1024]{0:T(1024)S(1)}, u32[]{:S(2)}) copy-start(s32[1024]{0:T(1024)S(1)} %pad_clamp_fusion.4) | copy-start | bytes 12292
  95.9 6.4 copy-start.43
  98.5 253.7 %all-reduce.22.cloned.1.call-start = ((), (), s32[]{:S(2)}) async-start(), calls=%async_computation.1 | async-start | bytes 393216
  102.3 78.6 %copy-start.75 = (pred[2,8]{1,0:T(4,128)(4,1)S(1)}, pred[2,8]{1,0:T(4,128)(4,1)}, u32[]{:S(2)}) copy-start(pred[2,8]{1,0:T(4,128)(4,1)} %get-tuple-element.206) | copy-start | bytes 52
  102.3 79.1 %copy-start.73 = (pred[2,8]{1,0:T(4,128)(4,1)S(1)}, pred[2,8]{1,0:T(4,128)(4,1)}, u32[]{:S(2)}) copy-start(pred[2,8]{1,0:T(4,128)(4,1)} %get-tuple-element.208) | copy-start | bytes 52
  102.3 79.7 %copy-start.71 = (pred[2,8]{1,0:T(4,128)(4,1)S(1)}, pred[2,8]{1,0:T(4,128)(4,1)}, u32[]{:S(2)}) copy-start(pred[2,8]{1,0:T(4,128)(4,1)} %get-tuple-element.207) | copy-start | bytes 52
  102.3 80.3 %copy-start.79 = (u32[128]{0:T(128)S(1)}, u32[128]{0:T(128)}, u32[]{:S(2)}) copy-start(u32[128]{0:T(128)} %constant.501) | copy-start | bytes 1540
  107.5 144.8 %copy-start.9 = (bf16[48,1536]{1,0:T(8,128)(2,1)S(1)}, bf16[48,1536]{1,0:T(8,128)(2,1)}, u32[]{:S(2)}) copy-start(bf16[48,1536]{1,0:T(8,128)(2,1)} %param.39) | copy-start | bytes 442372
  253.3 454.6 %all-reduce.24.cloned.1.call-start = ((), (), s32[]{:S(2)}) async-start(), calls=%async_computation.2 | async-start | bytes 3145728 | tf_op jit(solution)/shard_map/psum | solution.py:171
  456.8 26.4 %copy-start.69 = (pred[16]{0:T(512)(128)(4,1)S(1)}, pred[16]{0:T(512)(128)(4,1)}, u32[]{:S(2)}) copy-start(pred[16]{0:T(512)(128)(4,1)} %copy-done.68) | copy-start | bytes 52
  497.6 5.5 copy-start.41
  497.6 6.5 copy-start.50
  497.6 6.5 copy-start.36
  497.6 6.5 copy-start.37
  499.3 6.9 copy-start.21
  499.3 8.6 copy-start.18
  499.3 9.5 copy-start.19
  499.4 17.5 %copy-start.55 = (bf16[1,64,256]{2,1,0:T(8,128)(2,1)S(1)}, bf16[1,64,256]{2,1,0:T(8,128)(2,1)}, u32[]{:S(2)}) copy-start(bf16[1,64,256]{2,1,0:T(8,128)(2,1)} %get-tuple-element.151) | copy-start | bytes 98308
  505.4 13.1 %copy-start.25 = (bf16[4,64,256]{2,0,1:T(4,128)(2,1)}, bf16[4,64,256]{2,0,1:T(4,128)(2,1)S(1)}, u32[]{:S(2)}) copy-start(bf16[4,64,256]{2,0,1:T(4,128)(2,1)S(1)} %scatter.36) | copy-start | bytes 393220
  507.1 11.4 copy-start.22
  514.0 8.1 copy-start.58
  526.1 10.8 copy-start.33
  526.1 10.8 copy-start.35
  527.6 14.3 %copy-start.61 = (f32[16,2,6]{2,1,0:T(2,128)S(1)}, f32[16,2,6]{2,1,0:T(2,128)}, u32[]{:S(2)}) copy-start(f32[16,2,6]{2,1,0:T(2,128)} %copy.379) | copy-start | bytes 2308
  527.6 15.7 %copy-start.60 = (f32[16,2,6]{2,1,0:T(2,128)S(1)}, f32[16,2,6]{2,1,0:T(2,128)}, u32[]{:S(2)}) copy-start(f32[16,2,6]{2,1,0:T(2,128)} %copy.367) | copy-start | bytes 2308
  529.2 11.7 %copy-start.17 = (bf16[64,12,64]{2,0,1:T(8,128)(2,1)S(1)}, bf16[64,12,64]{2,0,1:T(8,128)(2,1)}, u32[]{:S(2)}) copy-start(bf16[64,12,64]{2,0,1:T(8,128)(2,1)} %copy.347) | copy-start | bytes 294916
  529.2 15.3 %copy-start.63 = (f32[16,2,6]{2,1,0:T(2,128)S(1)}, f32[16,2,6]{2,1,0:T(2,128)}, u32[]{:S(2)}) copy-start(f32[16,2,6]{2,1,0:T(2,128)} %copy.399) | copy-start | bytes 2308
  529.2 16.5 %copy-start.62 = (f32[16,2,6]{2,1,0:T(2,128)S(1)}, f32[16,2,6]{2,1,0:T(2,128)}, u32[]{:S(2)}) copy-start(f32[16,2,6]{2,1,0:T(2,128)} %copy.387) | copy-start | bytes 2308
  529.2 17.7 %copy-start.65 = (f32[16,2,6]{2,1,0:T(2,128)S(1)}, f32[16,2,6]{2,1,0:T(2,128)}, u32[]{:S(2)}) copy-start(f32[16,2,6]{2,1,0:T(2,128)} %copy.359) | copy-start | bytes 2308
  529.2 18.9 %copy-start.64 = (f32[16,2,6]{2,1,0:T(2,128)S(1)}, f32[16,2,6]{2,1,0:T(2,128)}, u32[]{:S(2)}) copy-start(f32[16,2,6]{2,1,0:T(2,128)} %copy.345) | copy-start | bytes 2308
  531.1 7.0 copy-start.30
  537.0 14.4 %copy-start.66 = (bf16[1,2,1536]{2,1,0:T(2,128)(2,1)S(1)}, bf16[1,2,1536]{2,1,0:T(2,128)(2,1)}, u32[]{:S(2)}) copy-start(bf16[1,2,1536]{2,1,0:T(2,128)(2,1)} %get-tuple-element.170) | copy-start | bytes 18436
  537.9 44.0 %copy-start.52 = (bf16[1,64,256]{2,0,1:T(2,128)(2,1)S(1)}, bf16[1,64,256]{2,0,1:T(2,128)(2,1)}, u32[]{:S(2)}) copy-start(bf16[1,64,256]{2,0,1:T(2,128)(2,1)} %copy.395) | copy-start | bytes 98308
  538.1 11.2 copy-start.27
  543.2 8.0 copy-start.11
  544.5 6.8 copy-start.12
  545.7 5.6 copy-start.13
  551.3 318.5 %all-reduce.26.cloned.1.call-start = ((), (), s32[]{:S(2)}) async-start(), calls=%async_computation.3 | async-start | bytes 12582912 | tf_op jit(solution)/shard_map/psum | solution.py:171
  585.8 284.0 %copy-start.29 = (bf16[4,64,256]{2,0,1:T(4,128)(2,1)S(1)}, bf16[4,64,256]{2,0,1:T(4,128)(2,1)}, u32[]{:S(2)}) copy-start(bf16[4,64,256]{2,0,1:T(4,128)(2,1)} %copy-done.28) | copy-start | bytes 393220
  585.8 395.1 %all-reduce.30.cloned.1.call-start = ((), (), s32[]{:S(2)}) async-start(), calls=%async_computation.5 | async-start | bytes 1179648
  587.9 283.4 %copy-start.57 = (f32[64,2,6,2]{2,3,1,0:T(2,128)}, f32[64,2,6,2]{2,3,1,0:T(2,128)S(1)}, u32[]{:S(2)}) copy-start(f32[64,2,6,2]{2,3,1,0:T(2,128)S(1)} %get-tuple-element.230) | copy-start | bytes 18436
  878.3 285.2 %all-reduce.28.cloned.1.call-start = ((), (), s32[]{:S(2)}) async-start(), calls=%async_computation.4 | async-start | bytes 1572864
  (38 other events, 119.1 us)
Sparse Core Ops, SparseCore 0:
  98.6 150.4 all-reduce.19
  253.5 98.6 all-reduce.21
  551.4 156.4 all-reduce.23
  713.0 156.7 all-reduce.25
  878.4 102.5 all-reduce.29
  1060.9 102.4 all-reduce.27
where the time goes:
time: 1180 us; the launch traced here: 1170 us
  waiting for transfers between devices  639 us (54%)
  blocking collectives  315 us (27%)
  local copies, waits for them, and re-layouts  95.5 us (8%)
  other arithmetic  53.3 us (5%)
  matrix products  52.6 us (4%)
  between operations  16.6 us (1%)
    psum x3, waiting for transfers between devices, per_device(): lax.psum((all_peak, all_total, all_output), ('req', 'tp'))  337 us
    unnamed x9, waiting for transfers between devices  302 us
    all_gather x4, blocking collectives, per_device(): piece = lax.all_gather(mixed_in, 'tp', axis=0, tiled=True)  102 us
    all_gather x4, blocking collectives, per_device(): lax.all_gather(normed, 'tp', axis=0, tiled=True)  99.2 us
    psum x1, blocking collectives, per_device(): lax.psum((all_peak, all_total, all_output), ('req', 'tp'))  67 us
    all_gather x4, blocking collectives, per_device(): lax.all_gather(queries.reshape(group_rows, attn_width), 'req', axis=0, ti...  46.6 us
  transfers between devices with their start and end apart: 6, of which 6 were waited for; matrix products, arithmetic and copies ran while one was open for 3% of the time, Pallas kernels for 0%

commit v1 on v0

--- a/solution.py
+++ b/solution.py
@@ -8,6 +8,12 @@
 theta_base = 1000000.0
 norm_eps = 1e-06
 masked_score = -1e30
+
+
+def tiled_gather(x, axis, dim):
+    peers = lax.axis_size(axis)
+    repeats = [peers if d == dim else 1 for d in range(x.ndim)]
+    return lax.all_to_all(jnp.tile(x, repeats), axis, split_axis=dim, concat_axis=dim, tiled=True)
 
 
 def rms_normed(values):
@@ -136,11 +142,7 @@
         inputs = step_inputs[step]
         normed = rms_normed(inputs)
         qkv = (
-            jnp.dot(
-                lax.all_gather(normed, "tp", axis=0, tiled=True),
-                qkv_weight,
-                preferred_element_type=jnp.float32,
-            )
+            jnp.dot(tiled_gather(normed, "tp", 0), qkv_weight, preferred_element_type=jnp.float32)
             + qkv_bias
         ).astype(jnp.bfloat16)
         my_roots = root_all[my_requests]

time: 1180 us -> 1150 us (0.975)
  blocking collectives: 315 us -> 214 us
  waiting for transfers between devices: 639 us -> 668 us
  starting transfers between devices: 0.42 us -> 24.8 us
    all_gather x4 -> x0, blocking collectives: 99.2 us -> none  [per_device(): lax.all_gather(normed, 'tp', axis=0, tiled=True)]
    psum x3, waiting for transfers between devices: 337 us -> 363 us  [per_device(): lax.psum((all_peak, all_total, all_output), ('req', 'tp'))]
    all_to_all x0 -> x4, starting transfers between devices: none -> 23.9 us  [tiled_gather(): lax.all_to_all(jnp.tile(x, repeats), axis, split_axis=dim, concat_axis=di...]
  transfers between devices with their start and end apart: 6 -> 10, of which waited for: 6 -> 8; matrix products, arithmetic and copies ran while one was open for 3% -> 9% of each run, Pallas kernels for 0% -> 0%
where the time goes in v1:
time: 1150 us; the launch traced here: 1140 us
  waiting for transfers between devices  668 us (58%)
  blocking collectives  214 us (19%)
  local copies, waits for them, and re-layouts  104 us (9%)
  other arithmetic  63.9 us (6%)
  matrix products  52.6 us (5%)
  starting transfers between devices  24.8 us (2%)
  between operations  16.3 us (1%)
    psum x3, waiting for transfers between devices, per_device(): lax.psum((all_peak, all_total, all_output), ('req', 'tp'))  363 us
    unnamed x9, waiting for transfers between devices  299 us
    all_gather x4, blocking collectives, per_device(): piece = lax.all_gather(mixed_in, 'tp', axis=0, tiled=True)  96.7 us
    psum x1, blocking collectives, per_device(): lax.psum((all_peak, all_total, all_output), ('req', 'tp'))  68.1 us
    all_gather x4, blocking collectives, per_device(): lax.all_gather(queries.reshape(group_rows, attn_width), 'req', axis=0, ti...  48.7 us
    all_to_all x4, starting transfers between devices, tiled_gather(): lax.all_to_all(jnp.tile(x, repeats), axis, split_axis=dim, concat_axis=di...  23.9 us
  transfers between devices with their start and end apart: 10, of which 8 were waited for; matrix products, arithmetic and copies ran while one was open for 9% of the time, Pallas kernels for 0%

profile of v1, /device:TPU:1, one launch (start us, length us, event | category | flops | bytes accessed | tf_op | source)
XLA Modules:
  0.0 1142.7 jit_solution(8045998785299604722)
XLA Ops:
  9.0 9.6 all-to-all-start
  21.8 1.9 gather_fusion.15
  24.1 1.9 gather_fusion.18
  27.5 1.9 gather_fusion.24
  30.3 1.9 gather_fusion.29
  44.5 7.0 reshape.1175
  51.6 6.9 reshape.1176
  65.0 4.0 fusion.28
  70.0 12.0 %all_gather.24 = bf16[256,1536]{1,0:T(8,128)(2,1)S(1)} all-gather(bf16[64,1536]{1,0:T(8,128)(2,1)S(1)} %bitcast.298), channel_id=1, replica_groups=mesh['req'=4,'tp'=32] {'req'}, dimensions={0}, use_global_device_ids=true | all-gather | bytes 983040 | tf_op jit(solution)/shard_map/all_gather | solution.py:157
  82.7 4.0 fusion.200
  92.4 2.7 fusion.20
  98.1 68.1 %all-reduce.9 = (f32[256,2,6]{0,1,2:T(2,128)S(1)}, f32[256,2,6]{0,1,2:T(2,128)S(1)}) all-reduce(f32[256,2,6]{0,1,2:T(2,128)S(1)} %copy.328, f32[256,2,6]{0,1,2:T(2,128)S(1)} %copy.335), channel_id=1, replica_groups=mesh['req'=4,'tp'=32] {'req','tp'}, use_global_device_ids=true, to_apply=%region_6.10 | all-reduce | flops 6144 | bytes 49152 | tf_op jit(solution)/shard_map/psum | solution.py:173
  166.9 77.4 %all-reduce.20.cloned.1.call-done = f32[256,2,6,128]{3,1,2,0:T(2,128)} async-done(((f32[256,2,6,128]{3,1,2,0:T(2,128)}), f32[256,2,6,128]{3,1,2,0:T(2,128)}) %all-reduce.20.cloned.1.call-update) | async-done | bytes 1572880 | tf_op jit(solution)/shard_map/psum | solution.py:173
  244.3 2.9 fusion.98
  251.9 95.5 %all-reduce.22.cloned.1.call-done = bf16[64,1536]{1,0:T(8,128)(2,1)} async-done(((bf16[64,1536]{1,0:T(8,128)(2,1)}), bf16[64,1536]{1,0:T(8,128)(2,1)}) %all-reduce.22.cloned.1.call-update) | async-done | bytes 196624
  349.9 5.5 all-to-all-start.2
  356.3 25.2 %all-gather = bf16[32,2,1536]{2,1,0:T(2,128)(2,1)S(1)} all-gather(bf16[1,2,1536]{2,1,0:T(2,128)(2,1)S(1)} %get-tuple-element.170), channel_id=1, replica_groups=mesh['req'=4,'tp'=32] {'tp'}, dimensions={0}, use_global_device_ids=true | all-gather | bytes 202752 | tf_op jit(solution)/shard_map/all_gather | solution.py:207
  382.4 4.8 all-to-all-start.1
  387.3 4.0 fusion.30
  392.0 3.5 all-to-all-done.1
  396.3 3.9 all-to-all-start.3
  400.7 4.0 fusion.29
  405.5 2.9 all-to-all-done.3
  408.5 4.0 fusion.31
  413.9 12.5 %all_gather.30 = bf16[256,1536]{1,0:T(8,128)(2,1)} all-gather(bf16[64,1536]{1,0:T(8,128)(2,1)S(1)} %bitcast.299), channel_id=1, replica_groups=mesh['req'=4,'tp'=32] {'req'}, dimensions={0}, use_global_device_ids=true | all-gather | bytes 983040 | tf_op jit(solution)/shard_map/all_gather | solution.py:157
  426.4 2.5 gather_fusion.31
  430.2 11.2 all_gather.26
  441.4 2.5 gather_fusion.20
  444.4 13.0 %all_gather.28 = bf16[256,1536]{1,0:T(8,128)(2,1)} all-gather(bf16[64,1536]{1,0:T(8,128)(2,1)S(1)} %bitcast.301), channel_id=1, replica_groups=mesh['req'=4,'tp'=32] {'req'}, dimensions={0}, use_global_device_ids=true | all-gather | bytes 983040 | tf_op jit(solution)/shard_map/all_gather | solution.py:157
  457.4 1.9 gather_fusion.26
  460.2 4.0 fusion.202
  471.0 1.7 fusion.93
  472.7 2.8 fusion.22
  495.3 2.3 scatter.41
  498.4 2.4 gather_fusion.32
  508.8 2.1 scatter_fusion.11
  511.8 2.1 scatter_fusion.10
  514.7 2.1 scatter_fusion.5
  517.5 2.1 scatter_fusion.4
  519.7 1.9 select_bitcast_fusion
  540.5 2.2 scatter.55
  546.6 131.7 %all-reduce.24.cloned.1.call-done = (f32[256,2,6]{2,1,0:T(2,128)}, f32[256,2,6]{2,1,0:T(2,128)}, f32[256,2,6]{2,1,0:T(2,128)}, f32[256,2,6]{2,1,0:T(2,128)}, f32[256,2,6]{2,1,0:T(2,128)}, /*index=5*/f32[256,2,6]{2,1,0:T(2,128)}) async-done(((f32[256,2,6]{2,1,0:T(2,128)}, f32[256,2,6]{2,1,0:T(2,128)}, f32[256,2,6]{2,1,0:T(2,128)}, f32[256,2,6]{2,1,0:T(2,128)}, f32[256,2,6]{2,1,0:T(2,128)}, ...) | async-done | bytes 73744 | tf_op jit(solution)/shard_map/psum | solution.py:173
  686.3 153.9 %all-reduce.26.cloned.1.call-done = (f32[256,2,6,128]{3,2,1,0:T(8,128)}, f32[256,2,6,128]{3,2,1,0:T(8,128)}, f32[256,2,6,128]{3,2,1,0:T(8,128)}) async-done(((f32[256,2,6,128]{3,2,1,0:T(8,128)}, f32[256,2,6,128]{3,2,1,0:T(8,128)}, f32[256,2,6,128]{3,2,1,0:T(8,128)}), (f32[256,2,6,128]{3,2,1,0:T(8,128)}, f32[256,2,6,128]{3,2,1,0:T(8,128)}, f32[256,2,6,128]{3,2,1,0:T(8,128)})) %all-reduce.26.cloned.1.call-update) | async-done | bytes 4718608 | tf_op jit(solution)/shard_map/psum | solution.py:173
  850.8 100.5 %all-reduce.30.cloned.1.call-done = (bf16[64,1536]{1,0:T(8,128)(2,1)}, bf16[64,1536]{1,0:T(8,128)(2,1)}, bf16[64,1536]{1,0:T(8,128)(2,1)}) async-done(((bf16[64,1536]{1,0:T(8,128)(2,1)}, bf16[64,1536]{1,0:T(8,128)(2,1)}, bf16[64,1536]{1,0:T(8,128)(2,1)}), (bf16[64,1536]{1,0:T(8,128)(2,1)}, bf16[64,1536]{1,0:T(8,128)(2,1)}, bf16[64,1536]{1,0:T(8,128)(2,1)})) %all-reduce.30.cloned.1.call-update) | async-done | bytes 589840
  953.2 24.9 %all-gather.1 = bf16[32,2,1536]{2,1,0:T(2,128)(2,1)S(1)} all-gather(bf16[1,2,1536]{2,1,0:T(2,128)(2,1)S(1)} %get-tuple-element.174), channel_id=1, replica_groups=mesh['req'=4,'tp'=32] {'tp'}, dimensions={0}, use_global_device_ids=true | all-gather | bytes 202752 | tf_op jit(solution)/shard_map/all_gather | solution.py:207
  980.2 22.5 %all-gather.2 = bf16[32,2,1536]{2,1,0:T(2,128)(2,1)S(1)} all-gather(bf16[1,2,1536]{2,1,0:T(2,128)(2,1)S(1)} %get-tuple-element.176), channel_id=1, replica_groups=mesh['req'=4,'tp'=32] {'tp'}, dimensions={0}, use_global_device_ids=true | all-gather | bytes 202752 | tf_op jit(solution)/shard_map/all_gather | solution.py:207
  1004.9 24.1 %all-gather.3 = bf16[32,2,1536]{2,1,0:T(2,128)(2,1)S(1)} all-gather(bf16[1,2,1536]{2,1,0:T(2,128)(2,1)S(1)} %get-tuple-element.175), channel_id=1, replica_groups=mesh['req'=4,'tp'=32] {'tp'}, dimensions={0}, use_global_device_ids=true | all-gather | bytes 202752 | tf_op jit(solution)/shard_map/all_gather | solution.py:207
  1031.2 102.6 %all-reduce.28.cloned.1.call-done = (bf16[64,1536]{1,0:T(8,128)(2,1)}, bf16[64,1536]{1,0:T(8,128)(2,1)}, bf16[64,1536]{1,0:T(8,128)(2,1)}, bf16[64,1536]{1,0:T(8,128)(2,1)}) async-done(((bf16[64,1536]{1,0:T(8,128)(2,1)}, bf16[64,1536]{1,0:T(8,128)(2,1)}, bf16[64,1536]{1,0:T(8,128)(2,1)}, bf16[64,1536]{1,0:T(8,128)(2,1)}), (bf16[64,1536]{1,0:T(8,128)(2,1)}, bf16[64,1536]{1,0:T(8,128)(2,1)}, ...) | async-done | bytes 786448
  (449 shorter events, 141.1 us)
Async XLA Ops:
  6.5 842.6 %copy-start = (bf16[280,1536]{1,0:T(8,128)(2,1)S(1)}, bf16[280,1536]{1,0:T(8,128)(2,1)}, u32[]{:S(2)}) copy-start(bf16[280,1536]{1,0:T(8,128)(2,1)} %param.42) | copy-start | bytes 2580484
  9.0 55.9 %all-to-all-start = ((bf16[32,2,1536]{2,1,0:T(2,128)(2,1)}), bf16[32,2,1536]{2,1,0:T(2,128)(2,1)S(1)}, u32[]{:S(2)}, u32[]{:S(2)}) async-start(bf16[32,2,1536]{2,1,0:T(2,128)(2,1)} %tile.8), calls=%async_computation | async-start | bytes 393216 | tf_op jit(solution)/shard_map/all_to_all | solution.py:16
  18.6 225.7 %all-reduce.20.cloned.1.call-start = ((), (), s32[]{:S(2)}) async-start(), calls=%async_computation.4 | async-start | bytes 3145728 | tf_op jit(solution)/shard_map/psum | solution.py:173
  20.9 61.7 %copy-start.50 = (pred[16]{0:T(512)(128)(4,1)}, pred[16]{0:T(512)(128)(4,1)S(1)}, u32[]{:S(2)}) copy-start(pred[16]{0:T(512)(128)(4,1)S(1)} %compare_and_fusion.4) | copy-start | bytes 52
  30.3 8.9 copy-start.2
  51.5 8.6 copy-start.58
  51.5 9.2 copy-start.56
  51.5 9.9 copy-start.54
  51.6 11.0 copy-start.61
  51.6 13.4 %copy-start.40 = (f32[2048]{0:T(1024)S(1)}, f32[2048]{0:T(1024)}, u32[]{:S(2)}) copy-start(f32[2048]{0:T(1024)} %param.38) | copy-start | bytes 24580
  59.4 9.6 copy-start.10
  91.5 255.9 %all-reduce.22.cloned.1.call-start = ((), (), s32[]{:S(2)}) async-start(), calls=%async_computation.5 | async-start | bytes 393216
  92.4 155.1 %copy-start.9 = (bf16[48,1536]{1,0:T(8,128)(2,1)S(1)}, bf16[48,1536]{1,0:T(8,128)(2,1)}, u32[]{:S(2)}) copy-start(bf16[48,1536]{1,0:T(8,128)(2,1)} %param.39) | copy-start | bytes 442372
  95.1 153.6 %copy-start.12 = (bf16[4,64,256]{2,0,1:T(4,128)(2,1)S(1)}, bf16[4,64,256]{2,0,1:T(4,128)(2,1)}, u32[]{:S(2)}) copy-start(bf16[4,64,256]{2,0,1:T(4,128)(2,1)} %copy-done.10) | copy-start | bytes 393220
  95.1 154.5 %copy-start.11 = (bf16[4,64,256]{2,0,1:T(4,128)(2,1)S(1)}, bf16[4,64,256]{2,0,1:T(4,128)(2,1)}, u32[]{:S(2)}) copy-start(bf16[4,64,256]{2,0,1:T(4,128)(2,1)} %copy-done.10) | copy-start | bytes 393220
  95.2 252.2 %copy-start.18 = (bf16[4,2,1536]{2,1,0:T(2,128)(2,1)S(1)}, bf16[4,2,1536]{2,1,0:T(2,128)(2,1)}, u32[]{:S(2)}) copy-start(bf16[4,2,1536]{2,1,0:T(2,128)(2,1)} %param.36) | copy-start | bytes 73732
  96.8 258.7 %copy-start.53 = (pred[64]{0:T(512)(128)(4,1)S(1)}, pred[64]{0:T(512)(128)(4,1)}, u32[]{:S(2)}) copy-start(pred[64]{0:T(512)(128)(4,1)} %get-tuple-element.245) | copy-start | bytes 196
  349.9 31.6 %all-to-all-start.2 = ((bf16[32,2,1536]{2,1,0:T(2,128)(2,1)}), bf16[32,2,1536]{2,1,0:T(2,128)(2,1)S(1)}, u32[]{:S(2)}, u32[]{:S(2)}) async-start(bf16[32,2,1536]{2,1,0:T(2,128)(2,1)} %tile.10), calls=%async_computation.2 | async-start | bytes 393216 | tf_op jit(solution)/shard_map/all_to_all | solution.py:16
  382.4 13.1 %all-to-all-start.1 = ((bf16[32,2,1536]{2,1,0:T(2,128)(2,1)}), bf16[32,2,1536]{2,1,0:T(2,128)(2,1)S(1)}, u32[]{:S(2)}, u32[]{:S(2)}) async-start(bf16[32,2,1536]{2,1,0:T(2,128)(2,1)} %tile.9), calls=%async_computation.1 | async-start | bytes 393216 | tf_op jit(solution)/shard_map/all_to_all | solution.py:16
  396.3 12.2 %all-to-all-start.3 = ((bf16[32,2,1536]{2,1,0:T(2,128)(2,1)}), bf16[32,2,1536]{2,1,0:T(2,128)(2,1)S(1)}, u32[]{:S(2)}, u32[]{:S(2)}) async-start(bf16[32,2,1536]{2,1,0:T(2,128)(2,1)} %tile.11), calls=%async_computation.3 | async-start | bytes 393216 | tf_op jit(solution)/shard_map/all_to_all | solution.py:16
  400.2 278.1 %all-reduce.24.cloned.1.call-start = ((), (), s32[]{:S(2)}) async-start(), calls=%async_computation.6 | async-start | bytes 3145728 | tf_op jit(solution)/shard_map/psum | solution.py:173
  408.5 4.8 copy-start.28
  408.5 4.8 copy-start.29
  413.8 30.1 %copy-start.32 = (f32[64,64]{1,0:T(8,128)S(1)}, f32[64,64]{1,0:T(8,128)}, u32[]{:S(2)}) copy-start(f32[64,64]{1,0:T(8,128)} %get-tuple-element.182) | copy-start | bytes 49156
  413.8 30.1 %copy-start.34 = (f32[64,64]{1,0:T(8,128)S(1)}, f32[64,64]{1,0:T(8,128)}, u32[]{:S(2)}) copy-start(f32[64,64]{1,0:T(8,128)} %get-tuple-element.183) | copy-start | bytes 49156
  430.1 29.1 %copy-start.51 = (pred[16]{0:T(512)(128)(4,1)S(1)}, pred[16]{0:T(512)(128)(4,1)}, u32[]{:S(2)}) copy-start(pred[16]{0:T(512)(128)(4,1)} %copy-done.50) | copy-start | bytes 52
  475.5 4.2 copy-start.30
  475.5 4.2 copy-start.31
  475.5 4.5 copy-start.43
  475.5 4.6 copy-start.22
  475.5 18.2 %copy-start.42 = (bf16[1,64,256]{2,1,0:T(8,128)(2,1)S(1)}, bf16[1,64,256]{2,1,0:T(8,128)(2,1)}, u32[]{:S(2)}) copy-start(bf16[1,64,256]{2,1,0:T(8,128)(2,1)} %get-tuple-element.151) | copy-start | bytes 98308
  478.6 41.0 %copy-start.52 = (pred[64]{0:T(512)(128)(4,1)S(1)}, pred[64]{0:T(512)(128)(4,1)}, u32[]{:S(2)}) copy-start(pred[64]{0:T(512)(128)(4,1)} %get-tuple-element.243) | copy-start | bytes 196
  481.0 22.2 %copy-start.23 = (bf16[4,64,256]{2,0,1:T(4,128)(2,1)}, bf16[4,64,256]{2,0,1:T(4,128)(2,1)S(1)}, u32[]{:S(2)}) copy-start(bf16[4,64,256]{2,0,1:T(4,128)(2,1)S(1)} %scatter.36) | copy-start | bytes 393220
  482.7 38.9 %copy-start.20 = (bf16[4,64,256]{2,0,1:T(4,128)(2,1)}, bf16[4,64,256]{2,0,1:T(4,128)(2,1)S(1)}, u32[]{:S(2)}) copy-start(bf16[4,64,256]{2,0,1:T(4,128)(2,1)S(1)} %scatter.40) | copy-start | bytes 393220
  498.4 6.4 copy-start.25
  504.8 16.9 %copy-start.44 = (bf16[64,2,64]{2,1,0:T(2,128)(2,1)S(1)}, bf16[64,2,64]{2,1,0:T(2,128)(2,1)}, u32[]{:S(2)}) copy-start(bf16[64,2,64]{2,1,0:T(2,128)(2,1)} %get-tuple-element.158) | copy-start | bytes 49156
  504.8 16.9 %copy-start.45 = (bf16[64,2,64]{2,1,0:T(2,128)(2,1)S(1)}, bf16[64,2,64]{2,1,0:T(2,128)(2,1)}, u32[]{:S(2)}) copy-start(bf16[64,2,64]{2,1,0:T(2,128)(2,1)} %get-tuple-element.159) | copy-start | bytes 49156
  506.4 15.1 %copy-start.13 = (f32[256,2,6]{2,1,0:T(2,128)}, f32[256,2,6]{2,1,0:T(2,128)S(1)}, u32[]{:S(2)}) copy-start(f32[256,2,6]{2,1,0:T(2,128)S(1)} %scatter_fusion.8) | copy-start | bytes 36868
  508.1 13.5 %copy-start.14 = (f32[256,2,6]{2,1,0:T(2,128)}, f32[256,2,6]{2,1,0:T(2,128)S(1)}, u32[]{:S(2)}) copy-start(f32[256,2,6]{2,1,0:T(2,128)S(1)} %scatter_fusion.7) | copy-start | bytes 36868
  521.6 4.9 copy-start.48
  521.6 318.6 %all-reduce.26.cloned.1.call-start = ((), (), s32[]{:S(2)}) async-start(), calls=%async_computation.7 | async-start | bytes 12582912 | tf_op jit(solution)/shard_map/psum | solution.py:173
  525.6 4.6 copy-start.46
  533.9 5.3 copy-start.16
  533.9 5.4 copy-start.17
  535.7 7.0 copy-start.19
  543.7 296.5 %copy-start.26 = (bf16[4,64,256]{2,0,1:T(4,128)(2,1)S(1)}, bf16[4,64,256]{2,0,1:T(4,128)(2,1)}, u32[]{:S(2)}) copy-start(bf16[4,64,256]{2,0,1:T(4,128)(2,1)} %copy-done.25) | copy-start | bytes 393220
  543.7 407.7 %all-reduce.30.cloned.1.call-start = ((), (), s32[]{:S(2)}) async-start(), calls=%async_computation.9 | async-start | bytes 1179648
  848.7 285.2 %all-reduce.28.cloned.1.call-start = ((), (), s32[]{:S(2)}) async-start(), calls=%async_computation.8 | async-start | bytes 1572864
  (24 other events, 64.2 us)
Sparse Core Ops, SparseCore 0:
  91.6 152.6 all-reduce.19
  248.6 98.6 all-reduce.21
  521.7 156.5 all-reduce.23
  683.4 156.7 all-reduce.25
  848.8 102.4 all-reduce.29
  1031.3 102.4 all-reduce.27
